TPU v7x, 128 devices: a whole 4x4x4 slice. The times are simulated.
128 devices in a mesh: ax: 8 (over x, core), ay: 16 (over z, y).
Axes of the slice: x: 4, y: 4, z: 4, core: 2. Of those that a mesh axis runs over, the one named last changes fastest.
Arguments:
- matrices: bfloat16 [2048, 512, 512], P(('ax', 'ay')), as said below
- basis_cols: bfloat16 [2048, 512, 384], P(('ax', 'ay')), may hold values from -6 to 6
- mode_counts: int32 [2048], P(('ax', 'ay')), may hold values from 64 to 384
- task_map: int32 [2048], P(('ax', 'ay')), may hold values from 0 to 15, as said below
- neighbour: int32 [2048], P(('ax', 'ay')), may hold values from 0 to 15
Outputs:
- smoothed: bfloat16 [2048, 512, 384], P(('ax', 'ay'))
- coarse: bfloat16 [2048, 384, 384], P(('ax', 'ay'))
Inputs may be any that keep to these rules, and one draw needn't show every extreme that they name: `task_map`: each block of 16 consecutive entries (the agglomerates of one device) holds every ay index exactly once. `matrices`: symmetric with a positive diagonal.
All inputs are finite; a program needn't handle non-finite values.
Results may differ from a plain program's by a relative error of at most 0.0066.
Values may be sent and summed in bfloat16 or wider, within the bound.
A program may use at most 128 MiB of HBM per device.

v0:
```python
import math

import jax
import jax.numpy as jnp
from jax import lax
from jax.sharding import PartitionSpec as P

TILE = 128


omegas = (0.3, 0.25, 0.2, 0.3, 0.25, 0.2)


def passed_along(block, axis, distance):
    devices = range(lax.axis_size(axis))
    route = [(i - distance, i) for i in devices if i - distance in devices]
    return lax.ppermute(block, axis, route)


def masked_columns(basis_cols, mode_counts):
    positions = lax.broadcasted_iota(jnp.int32, basis_cols.shape, 2)
    return jnp.where(positions < mode_counts[:, None, None], basis_cols, jnp.zeros_like(basis_cols))


def smooth_one(matrix, columns_in, live):

    def tile_step(tile, carry):
        result, applied = carry
        start = tile * TILE
        current = lax.dynamic_slice_in_dim(columns_in, start, TILE, 1)
        for weight in omegas:
            product = jnp.dot(matrix, current, preferred_element_type=jnp.float32)
            current = (current.astype(jnp.float32) - weight * product).astype(jnp.bfloat16)
        image = jnp.dot(matrix, current, preferred_element_type=jnp.float32).astype(jnp.bfloat16)
        result = lax.dynamic_update_slice_in_dim(result, current, start, 1)
        applied = lax.dynamic_update_slice_in_dim(applied, image, start, 1)
        return (result, applied)

    zeros = jnp.zeros(columns_in.shape, jnp.bfloat16)
    return lax.fori_loop(0, live, tile_step, (zeros, zeros))


def smooth_all(matrices, columns, live_counts):
    return lax.map(
        lambda item: smooth_one(item[0], item[1], item[2]), (matrices, columns, live_counts)
    )


def self_blocks(result, applied):
    return jnp.einsum("bum,bun->bmn", result, applied, preferred_element_type=jnp.float32)


def pair_terms(home_cols, home_image, neighbour):
    lower = passed_along(home_cols, "ax", 1)
    partner = jnp.take(lower, neighbour, axis=0)
    return jnp.einsum(
        "bum,bun->bmn", home_image, partner, preferred_element_type=jnp.float32
    ).astype(jnp.bfloat16)


def send_order(task_map):
    count = task_map.shape[0]
    positions = lax.broadcasted_iota(jnp.int32, (count, count), 1)
    slots = lax.broadcasted_iota(jnp.int32, (count, count), 0)
    return jnp.sum(jnp.where(task_map[:, None] == positions, slots, 0), axis=0)


def body(matrices, basis_cols, mode_counts, task_map, neighbour):
    width = matrices.shape[1]
    scale = 1.0 / math.sqrt(width)
    columns = masked_columns(basis_cols, mode_counts)
    order = send_order(task_map)
    tile_counts = (mode_counts + TILE - 1) // TILE
    home_cols, home_image = smooth_all(matrices, columns, tile_counts)
    own = self_blocks(home_cols, home_image)
    pair = pair_terms(home_cols, home_image, neighbour)
    finished = ((own + pair.astype(jnp.float32)) * scale).astype(jnp.bfloat16)
    coarse = lax.all_to_all(
        jnp.take(finished, order, axis=0), "ay", split_axis=0, concat_axis=0, tiled=True
    )
    return (home_cols, coarse)


def solution(mesh):
    placed = (
        P(("ax", "ay"), None, None),
        P(("ax", "ay"), None, None),
        P(("ax", "ay")),
        P(("ax", "ay")),
        P(("ax", "ay")),
    )
    return jax.shard_map(
        body,
        mesh=mesh,
        in_specs=placed,
        out_specs=(P(("ax", "ay"), None, None), P(("ax", "ay"), None, None)),
        check_vma=False,
    )
```

profile of v0, /device:TPU:4, one launch (start us, length us, event | category | flops | bytes accessed | tf_op | source)
XLA Modules:
  0.0 398.7 jit_solution(8628997871928530052)
XLA Ops:
  0.6 8.6 %copy.11 = bf16[16,512,384]{1,2,0:T(8,128)(2,1)} copy(bf16[16,512,384]{2,1,0:T(8,128)(2,1)} %param.10) | data formatting | bytes 12582912 | tf_op args[1]
  9.3 8.3 %fusion.22 = bf16[16,512,384]{1,2,0:T(8,128)(2,1)} fusion(bf16[16,512,384]{1,2,0:T(8,128)(2,1)} %copy.11, s32[16]{0:T(128)S(1)} %copy-done), kind=kLoop, calls=%fused_computation.37 | loop fusion | flops 6291456 | bytes 12582976 | tf_op jit(solution)/shard_map/jit(_where)/select_n | solution.py:22
  17.6 3.3 broadcast.86
  20.9 3.3 broadcast.86.clone
  24.3 162.7 %while.25 = (s32[]{:T(128)}, bf16[16,512,384]{1,2,0:T(8,128)(2,1)}, bf16[16,512,384]{1,2,0:T(8,128)(2,1)}, s32[16]{0:T(128)S(1)}, bf16[16,512,384]{1,2,0:T(8,128...) while((s32[]{:T(128)}, bf16[16,512,384]{1,2,0:T(8,128)(2,1)}, ...), condition=%wide.region_3.4_spmd, body=%wide.region_0.0_spmd.sunk | while | flops 471400448 | bytes 10094472 | solution.py:44
  24.3 1.1 dynamic-slice_bitcast_fusion.5
  25.4 1.0 dynamic-slice_bitcast_fusion.4
  27.0 6.1 %while.26 = (s32[]{:T(128)}, bf16[512,384]{0,1:T(8,128)(2,1)S(1)}, bf16[512,384]{0,1:T(8,128)(2,1)S(1)}, s32[]{:T(128)}, bf16[512,384]{0,1:T(8,128)(2,1)S(1)}, /...) while((s32[]{:T(128)}, bf16[512,384]{0,1:T(8,128)(2,1)S(1)}, ...), condition=%wide.region_2.2_spmd, body=%wide.region_1.1_spmd.sunk | while | flops 471400448 | bytes 5899419 | solution.py:40
  34.1 1.1 dynamic-slice_bitcast_fusion.5
  35.2 1.0 dynamic-slice_bitcast_fusion.4
  36.8 6.1 %while.26 = (s32[]{:T(128)}, bf16[512,384]{0,1:T(8,128)(2,1)S(1)}, bf16[512,384]{0,1:T(8,128)(2,1)S(1)}, s32[]{:T(128)}, bf16[512,384]{0,1:T(8,128)(2,1)S(1)}, /...) while((s32[]{:T(128)}, bf16[512,384]{0,1:T(8,128)(2,1)S(1)}, ...), condition=%wide.region_2.2_spmd, body=%wide.region_1.1_spmd.sunk | while | flops 471400448 | bytes 5899419 | solution.py:40
  43.9 1.1 dynamic-slice_bitcast_fusion.5
  45.0 1.0 dynamic-slice_bitcast_fusion.4
  46.6 3.3 while.26
  50.9 1.1 dynamic-slice_bitcast_fusion.5
  52.0 1.0 dynamic-slice_bitcast_fusion.4
  53.7 6.1 %while.26 = (s32[]{:T(128)}, bf16[512,384]{0,1:T(8,128)(2,1)S(1)}, bf16[512,384]{0,1:T(8,128)(2,1)S(1)}, s32[]{:T(128)}, bf16[512,384]{0,1:T(8,128)(2,1)S(1)}, /...) while((s32[]{:T(128)}, bf16[512,384]{0,1:T(8,128)(2,1)S(1)}, ...), condition=%wide.region_2.2_spmd, body=%wide.region_1.1_spmd.sunk | while | flops 471400448 | bytes 5899419 | solution.py:40
  60.7 1.1 dynamic-slice_bitcast_fusion.5
  61.8 1.0 dynamic-slice_bitcast_fusion.4
  63.5 8.9 %while.26 = (s32[]{:T(128)}, bf16[512,384]{0,1:T(8,128)(2,1)S(1)}, bf16[512,384]{0,1:T(8,128)(2,1)S(1)}, s32[]{:T(128)}, bf16[512,384]{0,1:T(8,128)(2,1)S(1)}, /...) while((s32[]{:T(128)}, bf16[512,384]{0,1:T(8,128)(2,1)S(1)}, ...), condition=%wide.region_2.2_spmd, body=%wide.region_1.1_spmd.sunk | while | flops 471400448 | bytes 5899419 | solution.py:40
  73.3 1.1 dynamic-slice_bitcast_fusion.5
  74.4 1.0 dynamic-slice_bitcast_fusion.4
  76.1 6.1 %while.26 = (s32[]{:T(128)}, bf16[512,384]{0,1:T(8,128)(2,1)S(1)}, bf16[512,384]{0,1:T(8,128)(2,1)S(1)}, s32[]{:T(128)}, bf16[512,384]{0,1:T(8,128)(2,1)S(1)}, /...) while((s32[]{:T(128)}, bf16[512,384]{0,1:T(8,128)(2,1)S(1)}, ...), condition=%wide.region_2.2_spmd, body=%wide.region_1.1_spmd.sunk | while | flops 471400448 | bytes 5899419 | solution.py:40
  83.1 1.1 dynamic-slice_bitcast_fusion.5
  84.2 1.0 dynamic-slice_bitcast_fusion.4
  85.9 6.1 %while.26 = (s32[]{:T(128)}, bf16[512,384]{0,1:T(8,128)(2,1)S(1)}, bf16[512,384]{0,1:T(8,128)(2,1)S(1)}, s32[]{:T(128)}, bf16[512,384]{0,1:T(8,128)(2,1)S(1)}, /...) while((s32[]{:T(128)}, bf16[512,384]{0,1:T(8,128)(2,1)S(1)}, ...), condition=%wide.region_2.2_spmd, body=%wide.region_1.1_spmd.sunk | while | flops 471400448 | bytes 5899419 | solution.py:40
  92.9 1.1 dynamic-slice_bitcast_fusion.5
  94.0 1.0 dynamic-slice_bitcast_fusion.4
  95.7 3.3 while.26
  100.0 1.1 dynamic-slice_bitcast_fusion.5
  101.1 1.0 dynamic-slice_bitcast_fusion.4
  102.7 3.3 while.26
  107.1 1.1 dynamic-slice_bitcast_fusion.5
  108.1 1.0 dynamic-slice_bitcast_fusion.4
  109.8 6.1 %while.26 = (s32[]{:T(128)}, bf16[512,384]{0,1:T(8,128)(2,1)S(1)}, bf16[512,384]{0,1:T(8,128)(2,1)S(1)}, s32[]{:T(128)}, bf16[512,384]{0,1:T(8,128)(2,1)S(1)}, /...) while((s32[]{:T(128)}, bf16[512,384]{0,1:T(8,128)(2,1)S(1)}, ...), condition=%wide.region_2.2_spmd, body=%wide.region_1.1_spmd.sunk | while | flops 471400448 | bytes 5899419 | solution.py:40
  116.9 1.1 dynamic-slice_bitcast_fusion.5
  118.0 1.0 dynamic-slice_bitcast_fusion.4
  119.6 8.9 %while.26 = (s32[]{:T(128)}, bf16[512,384]{0,1:T(8,128)(2,1)S(1)}, bf16[512,384]{0,1:T(8,128)(2,1)S(1)}, s32[]{:T(128)}, bf16[512,384]{0,1:T(8,128)(2,1)S(1)}, /...) while((s32[]{:T(128)}, bf16[512,384]{0,1:T(8,128)(2,1)S(1)}, ...), condition=%wide.region_2.2_spmd, body=%wide.region_1.1_spmd.sunk | while | flops 471400448 | bytes 5899419 | solution.py:40
  129.5 1.1 dynamic-slice_bitcast_fusion.5
  130.6 1.0 dynamic-slice_bitcast_fusion.4
  132.3 8.9 %while.26 = (s32[]{:T(128)}, bf16[512,384]{0,1:T(8,128)(2,1)S(1)}, bf16[512,384]{0,1:T(8,128)(2,1)S(1)}, s32[]{:T(128)}, bf16[512,384]{0,1:T(8,128)(2,1)S(1)}, /...) while((s32[]{:T(128)}, bf16[512,384]{0,1:T(8,128)(2,1)S(1)}, ...), condition=%wide.region_2.2_spmd, body=%wide.region_1.1_spmd.sunk | while | flops 471400448 | bytes 5899419 | solution.py:40
  142.1 1.1 dynamic-slice_bitcast_fusion.5
  143.2 1.0 dynamic-slice_bitcast_fusion.4
  144.9 6.1 %while.26 = (s32[]{:T(128)}, bf16[512,384]{0,1:T(8,128)(2,1)S(1)}, bf16[512,384]{0,1:T(8,128)(2,1)S(1)}, s32[]{:T(128)}, bf16[512,384]{0,1:T(8,128)(2,1)S(1)}, /...) while((s32[]{:T(128)}, bf16[512,384]{0,1:T(8,128)(2,1)S(1)}, ...), condition=%wide.region_2.2_spmd, body=%wide.region_1.1_spmd.sunk | while | flops 471400448 | bytes 5899419 | solution.py:40
  151.9 1.1 dynamic-slice_bitcast_fusion.5
  153.0 1.0 dynamic-slice_bitcast_fusion.4
  154.7 8.9 %while.26 = (s32[]{:T(128)}, bf16[512,384]{0,1:T(8,128)(2,1)S(1)}, bf16[512,384]{0,1:T(8,128)(2,1)S(1)}, s32[]{:T(128)}, bf16[512,384]{0,1:T(8,128)(2,1)S(1)}, /...) while((s32[]{:T(128)}, bf16[512,384]{0,1:T(8,128)(2,1)S(1)}, ...), condition=%wide.region_2.2_spmd, body=%wide.region_1.1_spmd.sunk | while | flops 471400448 | bytes 5899419 | solution.py:40
  164.5 1.1 dynamic-slice_bitcast_fusion.5
  165.6 1.0 dynamic-slice_bitcast_fusion.4
  167.3 8.9 %while.26 = (s32[]{:T(128)}, bf16[512,384]{0,1:T(8,128)(2,1)S(1)}, bf16[512,384]{0,1:T(8,128)(2,1)S(1)}, s32[]{:T(128)}, bf16[512,384]{0,1:T(8,128)(2,1)S(1)}, /...) while((s32[]{:T(128)}, bf16[512,384]{0,1:T(8,128)(2,1)S(1)}, ...), condition=%wide.region_2.2_spmd, body=%wide.region_1.1_spmd.sunk | while | flops 471400448 | bytes 5899419 | solution.py:40
  177.2 1.1 dynamic-slice_bitcast_fusion.5
  178.2 1.0 dynamic-slice_bitcast_fusion.4
  179.9 6.1 %while.26 = (s32[]{:T(128)}, bf16[512,384]{0,1:T(8,128)(2,1)S(1)}, bf16[512,384]{0,1:T(8,128)(2,1)S(1)}, s32[]{:T(128)}, bf16[512,384]{0,1:T(8,128)(2,1)S(1)}, /...) while((s32[]{:T(128)}, bf16[512,384]{0,1:T(8,128)(2,1)S(1)}, ...), condition=%wide.region_2.2_spmd, body=%wide.region_1.1_spmd.sunk | while | flops 471400448 | bytes 5899419 | solution.py:40
  187.0 2.1 collective-permute-start
  189.2 11.7 %fusion.31 = f32[16,384,384]{2,1,0:T(8,128)} fusion(bf16[16,512,384]{1,2,0:T(8,128)(2,1)} %get-tuple-element.73, bf16[16,512,384]{1,2,0:T(8,128)(2,1)} %get-tuple-element.70), kind=kOutput, calls=%fused_computation.59 | convolution fusion | flops 2415919104 | bytes 22020096 | tf_op jit(solution)/shard_map/bum,bun->bmn/dot_general | solution.py:50
  200.9 58.7 %collective-permute-done = bf16[16,512,384]{1,2,0:T(8,128)(2,1)} collective-permute-done((bf16[16,512,384]{1,2,0:T(8,128)(2,1)}, bf16[16,512,384]{1,2,0:T(8,128)(2,1)}, u32[]{:S(2)}, u32[]{:S(2)}) %collective-permute-start) | collective-permute-done | bytes 6291488 | tf_op jit(solution)/shard_map/ppermute | solution.py:17
  259.6 6.4 %gather_fusion = bf16[16,512,384]{1,2,0:T(8,128)(2,1)} fusion(bf16[16,512,384]{1,2,0:T(8,128)(2,1)} %collective-permute-done, s32[1024]{0:T(1024)S(1)} %pad_clamp_fusion.1), kind=kCustom, calls=%fused_computation | custom fusion | bytes 12582976 | tf_op jit(solution)/shard_map/jit(_take)/gather | solution.py:55
  265.9 13.0 %multiply_convert_fusion = bf16[16,384,384]{2,1,0:T(8,128)(2,1)} fusion(f32[16,384,384]{2,1,0:T(8,128)} %fusion.31, bf16[16,512,384]{1,2,0:T(8,128)(2,1)} %get-tuple-element.70, bf16[16,512,384]{1,2,0:T(8,128)(2,1)} %gather_fusion, pred[16]{0:T(512)(128)(4,1)S(1)} %compare_and_fusion), kind=kOutput, calls=%fused_computation.38 | convolution fusion | flops 2430861312 | bytes 26738704 | tf_op jit(solution)/shard_map/bum,bun->bmn/dot_general | solution.py:56
  278.9 5.7 %gather_fusion.1 = bf16[16,384,384]{2,1,0:T(8,128)(2,1)} fusion(bf16[16,384,384]{2,1,0:T(8,128)(2,1)} %multiply_convert_fusion, s32[1024]{0:T(1024)S(1)} %pad_clamp_fusion), kind=kCustom, calls=%fused_computation.1 | custom fusion | bytes 9437248 | tf_op jit(solution)/shard_map/jit(_take)/gather | solution.py:79
  284.6 5.1 %broadcast_select_fusion = bf16[16,384,384]{2,1,0:T(8,128)(2,1)} fusion(bf16[16,384,384]{2,1,0:T(8,128)(2,1)} %gather_fusion.1, pred[16]{0:T(512)(128)(4,1)S(1)} %compare_and_fusion.1), kind=kLoop, calls=%fused_computation.42 | loop fusion | flops 2359296 | bytes 9437200 | tf_op jit(solution)/shard_map/jit(_take)/select_n | solution.py:79
  289.8 35.1 %all-to-all-start = ((bf16[16,384,384]{2,1,0:T(8,128)(2,1)}), bf16[16,384,384]{2,1,0:T(8,128)(2,1)}, u32[]{:S(2)}, u32[]{:S(2)}) async-start(bf16[16,384,384]{2,1,0:T(8,128)(2,1)} %broadcast_select_fusion), calls=%async_computation | async-start | bytes 9437184 | tf_op jit(solution)/shard_map/all_to_all | solution.py:78
  324.9 8.6 %copy.14 = bf16[16,512,384]{2,1,0:T(8,128)(2,1)} copy(bf16[16,512,384]{1,2,0:T(8,128)(2,1)} %get-tuple-element.73) | data formatting | bytes 12582912
  333.5 60.0 %all-to-all-done = bf16[16,384,384]{2,1,0:T(8,128)(2,1)} async-done(((bf16[16,384,384]{2,1,0:T(8,128)(2,1)}), bf16[16,384,384]{2,1,0:T(8,128)(2,1)}, u32[]{:S(2)}, u32[]{:S(2)}) %all-to-all-start) | async-done | bytes 4718624 | tf_op jit(solution)/shard_map/all_to_all | solution.py:78
  393.5 5.1 %copy.43 = bf16[16,384,384]{2,1,0:T(8,128)(2,1)} copy(bf16[16,384,384]{2,1,0:T(8,128)(2,1)} %all-to-all-done) | data formatting | bytes 9437184
  (316 shorter events, 98.8 us)
Async XLA Ops:
  0.6 8.6 %copy-start = (s32[16]{0:T(128)S(1)}, s32[16]{0:T(128)}, u32[]{:S(2)}) copy-start(s32[16]{0:T(128)} %param.11) | copy-start | bytes 196
  24.2 164.8 %copy-start.2 = (s32[16]{0:T(128)S(1)}, s32[16]{0:T(128)}, u32[]{:S(2)}) copy-start(s32[16]{0:T(128)} %param.13) | copy-start | bytes 196
  24.2 164.8 %copy-start.1 = (s32[16]{0:T(128)S(1)}, s32[16]{0:T(128)}, u32[]{:S(2)}) copy-start(s32[16]{0:T(128)} %param.12) | copy-start | bytes 196
  187.0 72.6 %collective-permute-start = (bf16[16,512,384]{1,2,0:T(8,128)(2,1)}, bf16[16,512,384]{1,2,0:T(8,128)(2,1)}, u32[]{:S(2)}, u32[]{:S(2)}) collective-permute-start(bf16[16,512,384]{1,2,0:T(8,128)(2,1)} %get-tuple-element.73), channel_id=1, source_target_pairs={{0,16},{16,32},{32,48},{48,64},{64,80},{80,96},{96,112},{1,17},{17... | collective-permute-start | bytes 18874376 | tf_op jit(solution)/shard_map/ppermute | solution.py:17
  289.8 103.8 %all-to-all-start = ((bf16[16,384,384]{2,1,0:T(8,128)(2,1)}), bf16[16,384,384]{2,1,0:T(8,128)(2,1)}, u32[]{:S(2)}, u32[]{:S(2)}) async-start(bf16[16,384,384]{2,1,0:T(8,128)(2,1)} %broadcast_select_fusion), calls=%async_computation | async-start | bytes 9437184 | tf_op jit(solution)/shard_map/all_to_all | solution.py:78
where the time goes:
time: 401 us; the launch traced here: 399 us
  waiting for transfers between devices  119 us (30%)
  local copies, waits for them, and re-layouts  99.9 us (25%)
  matrix products  98.2 us (24%)
  starting transfers between devices  37.2 us (9%)
  loops' own time  30.4 us (8%)
  other arithmetic  13.6 us (3%)
    dot_general x204, matrix products, tile_step(): product = jnp.dot(matrix, current, preferred_element_type=jnp.float32)  63.1 us
    all_to_all x1, waiting for transfers between devices, body(): lax.all_to_all(jnp.take(finished, order, axis=0), 'ay', split_axis=0, con...  60 us
    ppermute x1, waiting for transfers between devices, passed_along(): return lax.ppermute(block, axis, route)  58.7 us
    all_to_all x1, starting transfers between devices, body(): lax.all_to_all(jnp.take(finished, order, axis=0), 'ay', split_axis=0, con...  35.1 us
    squeeze x32, local copies, waits for them, and re-layouts, smooth_all(): lax.map(lambda item: smooth_one(item[0], item[1], item[2]), (matrices, co...  33.7 us
    another operation x16, loops' own time, smooth_one(): return lax.fori_loop(0, live, tile_step, (zeros, zeros))  30 us
    unnamed x9, local copies, waits for them, and re-layouts  22.4 us
    dynamic_update_slice x16, local copies, waits for them, and re-layouts, smooth_all(): lax.map(lambda item: smooth_one(item[0], item[1], item[2]), (matrices, co...  15.2 us
  transfers between devices with their start and end apart: 2, of which 2 were waited for; matrix products, arithmetic and copies ran while one was open for 5% of the time, Pallas kernels for 0%

commit v1 on v0

v1 whole, which is shorter than its diff:
```python
import math

import jax
import jax.numpy as jnp
from jax import lax
from jax.experimental import pallas as pl
from jax.experimental.pallas import tpu as pltpu
from jax.sharding import PartitionSpec as P

TILE = 128
GROUP = 4
SLOTS = 16
U = 512
M = 384

omegas = (0.3, 0.25, 0.2, 0.3, 0.25, 0.2)


def smooth_kernel(counts, a_ref, x_ref, s_ref, st_ref, it_ref):
    base = pl.program_id(0) * GROUP
    for start in range(0, M, TILE):
        cols = []
        for k in range(GROUP):
            place = start + lax.broadcasted_iota(jnp.int32, (U, TILE), 1)
            kept = x_ref[k, :, start : start + TILE].astype(jnp.float32)
            kept = jnp.where(place < counts[base + k], kept, 0.0)
            cols.append(kept.T.astype(jnp.bfloat16))
        for weight in omegas:
            products = [
                jnp.dot(cols[k], a_ref[k], preferred_element_type=jnp.float32)
                for k in range(GROUP)
            ]
            cols = [
                (cols[k].astype(jnp.float32) - weight * products[k]).astype(jnp.bfloat16)
                for k in range(GROUP)
            ]
        for k in range(GROUP):
            s_ref[k, :, start : start + TILE] = cols[k].T
            st_ref[k, start : start + TILE, :] = cols[k]
            image = jnp.dot(cols[k], a_ref[k], preferred_element_type=jnp.float32)
            it_ref[k, start : start + TILE, :] = image.astype(jnp.bfloat16)


def smooth_all(counts, matrices, basis_cols):
    whole = lambda *shape: pl.BlockSpec((GROUP,) + shape, lambda i, c: (i, 0, 0))
    return pl.pallas_call(
        smooth_kernel,
        grid_spec=pltpu.PrefetchScalarGridSpec(
            num_scalar_prefetch=1,
            grid=(SLOTS // GROUP,),
            in_specs=[whole(U, U), whole(U, M)],
            out_specs=[whole(U, M), whole(M, U), whole(M, U)],
        ),
        out_shape=[
            jax.ShapeDtypeStruct((SLOTS, U, M), jnp.bfloat16),
            jax.ShapeDtypeStruct((SLOTS, M, U), jnp.bfloat16),
            jax.ShapeDtypeStruct((SLOTS, M, U), jnp.bfloat16),
        ],
        compiler_params=pltpu.CompilerParams(vmem_limit_bytes=56 << 20),
    )(counts, matrices, basis_cols)


def block_kernel(order, neighbour, it_ref, st_ref, low_ref, out_ref):
    both = st_ref[0].astype(jnp.float32) + low_ref[0].astype(jnp.float32)
    total = lax.dot_general(
        it_ref[0],
        both.astype(jnp.bfloat16),
        (((1,), (1,)), ((), ())),
        preferred_element_type=jnp.float32,
    )
    out_ref[0] = (total * (1.0 / math.sqrt(U))).astype(jnp.bfloat16)


def blocks(order, neighbour, image_t, smoothed_t, lower_t):
    mine = pl.BlockSpec((1, M, U), lambda j, o, n: (o[j], 0, 0))
    return pl.pallas_call(
        block_kernel,
        grid_spec=pltpu.PrefetchScalarGridSpec(
            num_scalar_prefetch=2,
            grid=(SLOTS,),
            in_specs=[
                mine,
                mine,
                pl.BlockSpec((1, M, U), lambda j, o, n: (n[o[j]], 0, 0)),
            ],
            out_specs=pl.BlockSpec((1, M, M), lambda j, o, n: (j, 0, 0)),
        ),
        out_shape=jax.ShapeDtypeStruct((SLOTS, M, M), jnp.bfloat16),
    )(order, neighbour, image_t, smoothed_t, lower_t)


def send_order(task_map):
    positions = lax.broadcasted_iota(jnp.int32, (SLOTS, SLOTS), 1)
    slots = lax.broadcasted_iota(jnp.int32, (SLOTS, SLOTS), 0)
    return jnp.sum(jnp.where(task_map[:, None] == positions, slots, 0), axis=0)


def body(matrices, basis_cols, mode_counts, task_map, neighbour):
    order = send_order(task_map)
    smoothed, smoothed_t, image_t = smooth_all(mode_counts, matrices, basis_cols)
    lower_t = lax.ppermute(smoothed_t, "ax", [(i, i + 1) for i in range(7)])
    ready = blocks(order, neighbour, image_t, smoothed_t, lower_t)
    coarse = lax.all_to_all(ready, "ay", split_axis=0, concat_axis=0, tiled=True)
    return smoothed, coarse


def solution(mesh):
    split = P(("ax", "ay"))
    return jax.shard_map(
        body,
        mesh=mesh,
        in_specs=(split,) * 5,
        out_specs=(split, split),
        check_vma=False,
    )
```

time: 401 us -> 186 us (0.46)
  matrix products: 98.2 us -> 0 us
  local copies, waits for them, and re-layouts: 99.9 us -> 2.19 us
  blocking collectives: 0 us -> 64.5 us
  waiting for transfers between devices: 119 us -> 70.1 us
  Pallas kernels: 0 us -> 46 us
  starting transfers between devices: 37.2 us -> 1.91 us
  loops' own time: 30.4 us -> 0 us
  other arithmetic: 13.6 us -> 0.6 us
    dot_general x240 -> x0, matrix products: 98.2 us -> none  [the longest x204 63.1 us: tile_step(): product = jnp.dot(matrix, current, preferred_element_type=jnp.float32)]
    all_to_all x0 -> x1, blocking collectives: none -> 64.5 us  [body(): lax.all_to_all(ready, 'ay', split_axis=0, concat_axis=0, tiled=True)]
    all_to_all x1 -> x0, waiting for transfers between devices: 60 us -> none  [body(): lax.all_to_all(jnp.take(finished, order, axis=0), 'ay', split_axis=0, con...]
    pallas_call x0 -> x2, Pallas kernels: none -> 46 us  [the longest x1 29.4 us: smooth_all(): pl.pallas_call(smooth_kernel, grid_spec=pltpu.PrefetchScalarGridSpec(num_...]
    all_to_all x1 -> x0, starting transfers between devices: 35.1 us -> none  [body(): lax.all_to_all(jnp.take(finished, order, axis=0), 'ay', split_axis=0, con...]
    squeeze x32 -> x0, local copies, waits for them, and re-layouts: 33.7 us -> none  [smooth_all(): lax.map(lambda item: smooth_one(item[0], item[1], item[2]), (matrices, co...]
    another operation x17 -> x0, loops' own time: 30.4 us -> none  [the longest x16 30 us: smooth_one(): return lax.fori_loop(0, live, tile_step, (zeros, zeros))]
    unnamed x9 -> x3, local copies, waits for them, and re-layouts: 22.4 us -> 2.19 us
  transfers between devices with their start and end apart: 2 -> 1, of which waited for: 2 -> 1; matrix products, arithmetic and copies ran while one was open for 5% -> 0% of each run, Pallas kernels for 0% -> 0%
where the time goes in v1:
time: 186 us
  waiting for transfers between devices  70.1 us (38%)
  blocking collectives  64.5 us (35%)
  Pallas kernels  46 us (25%)
  local copies, waits for them, and re-layouts  2.19 us (1%)
  starting transfers between devices  1.91 us (1%)
    ppermute x1, waiting for transfers between devices, body(): lower_t = lax.ppermute(smoothed_t, 'ax', [(i, i + 1) for i in range(7)])  70.1 us
    all_to_all x1, blocking collectives, body(): lax.all_to_all(ready, 'ay', split_axis=0, concat_axis=0, tiled=True)  64.5 us
    pallas_call x1, Pallas kernels, smooth_all(): pl.pallas_call(smooth_kernel, grid_spec=pltpu.PrefetchScalarGridSpec(num_...  29.4 us
    pallas_call x1, Pallas kernels, blocks(): pl.pallas_call(block_kernel, grid_spec=pltpu.PrefetchScalarGridSpec(num_s...  16.5 us
  transfers between devices with their start and end apart: 1, of which 1 were waited for; matrix products, arithmetic and copies ran while one was open for 0% of the time, Pallas kernels for 0%

profile of v1, /device:TPU:4, one launch (start us, length us, event | category | flops | bytes accessed | tf_op | source)
XLA Modules:
  0.0 185.9 jit_solution(4964995685565983878)
XLA Ops:
  0.6 0.0 copy-start
  0.6 29.4 %shard_map.68 = (bf16[16,512,384]{2,1,0:T(8,128)(2,1)}, bf16[16,384,512]{2,1,0:T(8,128)(2,1)}, bf16[16,384,512]{2,1,0:T(8,128)(2,1)}) custom-call(s32[16]{0:T(128)} %counts.1, bf16[16,512,512]{2,1,0:T(8,128)(2,1)} %a_ref.1, bf16[16,512,384]{2,1,0:T(8,128)(2,1)} %x_ref.1), custom_call_target="tpu_custom_call" | custom-call | tf_op jit(solution)/shard_map/pallas_call | solution.py:46
  30.1 1.9 %collective-permute-start = (bf16[16,384,512]{2,1,0:T(8,128)(2,1)}, bf16[16,384,512]{2,1,0:T(8,128)(2,1)}, u32[]{:S(2)}, u32[]{:S(2)}) collective-permute-start(bf16[16,384,512]{2,1,0:T(8,128)(2,1)} %get-tuple-element.7.st_ref), channel_id=1, source_target_pairs={{0,16},{16,32},{32,48},{48,64},{64,80},{80,96},{96,112},{1,17},{17... | collective-permute-start | bytes 18874376 | tf_op jit(solution)/shard_map/ppermute | solution.py:101
  32.0 0.0 copy-done
  32.0 0.6 select_reduce_fusion.order
  32.6 70.1 %collective-permute-done.low_ref = bf16[16,384,512]{2,1,0:T(8,128)(2,1)} collective-permute-done((bf16[16,384,512]{2,1,0:T(8,128)(2,1)}, bf16[16,384,512]{2,1,0:T(8,128)(2,1)}, u32[]{:S(2)}, u32[]{:S(2)}) %collective-permute-start) | collective-permute-done | bytes 6291488 | tf_op jit(solution)/shard_map/ppermute | solution.py:101
  102.7 16.5 %shard_map.69 = bf16[16,384,384]{2,1,0:T(8,128)(2,1)} custom-call(s32[16]{0:T(128)} %select_reduce_fusion.order, s32[16]{0:T(128)} %neighbour.1, bf16[16,384,512]{2,1,0:T(8,128)(2,1)} %get-tuple-element.6.it_ref, bf16[16,384,512]{2,1,0:T(8,128)(2,1)} %get-tuple-element.7.st_ref, bf16[16,384,512]{2,1,0:T(8,128)(2,1)} %collective-permute-done.low_ref), custom_call_target="tpu_custom_call" | custom-call | tf_op jit(solution)/shard_map/pallas_call | solution.py:76
  119.2 64.5 %all_to_all.5 = bf16[16,384,384]{2,1,0:T(8,128)(2,1)S(1)} all-to-all(bf16[16,384,384]{2,1,0:T(8,128)(2,1)} %shard_map.69), channel_id=1, replica_groups=mesh['ax'=8,'ay'=16] {'ay'}, dimensions={0} | all-to-all | bytes 9437184 | tf_op jit(solution)/shard_map/all_to_all | solution.py:103
  183.7 2.2 %copy.8 = bf16[16,384,384]{2,1,0:T(8,128)(2,1)} copy(bf16[16,384,384]{2,1,0:T(8,128)(2,1)S(1)} %all_to_all.5) | data formatting | bytes 9437184
Async XLA Ops:
  0.6 31.4 %copy-start = (s32[16]{0:T(128)S(1)}, s32[16]{0:T(128)}, u32[]{:S(2)}) copy-start(s32[16]{0:T(128)} %param.8) | copy-start | bytes 196
  30.1 72.6 %collective-permute-start = (bf16[16,384,512]{2,1,0:T(8,128)(2,1)}, bf16[16,384,512]{2,1,0:T(8,128)(2,1)}, u32[]{:S(2)}, u32[]{:S(2)}) collective-permute-start(bf16[16,384,512]{2,1,0:T(8,128)(2,1)} %get-tuple-element.7.st_ref), channel_id=1, source_target_pairs={{0,16},{16,32},{32,48},{48,64},{64,80},{80,96},{96,112},{1,17},{17... | collective-permute-start | bytes 18874376 | tf_op jit(solution)/shard_map/ppermute | solution.py:101

commit v2 on v1

v2 whole, which is shorter than its diff:
```python
import math

import jax
import jax.numpy as jnp
from jax import lax
from jax.experimental import pallas as pl
from jax.experimental.pallas import tpu as pltpu
from jax.sharding import PartitionSpec as P

TILE = 128
TILES = 3
GROUP = 4
GROUPS = 4
SLOTS = 16
U = 512
M = 384
ROWS = 8
MESH = pl.DeviceIdType.MESH

omegas = (0.3, 0.25, 0.2, 0.3, 0.25, 0.2)


def lanes(t):
    return pl.ds(pl.multiple_of(t * TILE, TILE), TILE)


def remote(src, dst, send_sem, recv_sem, where):
    return pltpu.make_async_remote_copy(
        src_ref=src,
        dst_ref=dst,
        send_sem=send_sem,
        recv_sem=recv_sem,
        device_id=where,
        device_id_type=MESH,
    )


def kernel(
    counts, task_map, neighbour, a_hbm, x_hbm, smoothed, coarse,
    a, x, image, low0, low1, low2, ready,
    a_sem, x_sem, up_send, up_recv, out_send, out_recv, own_sem,
):
    lows = (low0, low1, low2)
    row = lax.axis_index("ax")
    me = lax.axis_index("ay")
    up = lax.rem(row + 1, ROWS)
    fast = jnp.logical_or(lax.rem(row, 2) == 1, row == 0)
    slow = jnp.logical_not(fast)

    barrier = pltpu.get_barrier_semaphore()
    for k in range(1, SLOTS):
        pl.semaphore_signal(
            barrier, inc=1, device_id={"ay": lax.rem(me + k, SLOTS)}, device_id_type=MESH
        )
    for k in (1, ROWS - 1):
        pl.semaphore_signal(
            barrier, inc=1, device_id={"ax": lax.rem(row + k, ROWS)}, device_id_type=MESH
        )

    def a_load(g):
        part = pl.ds(g * GROUP, GROUP)
        return pltpu.make_async_copy(a_hbm.at[part], a.at[part], a_sem.at[g])

    def x_load(t, g):
        part = pl.ds(g * GROUP, GROUP)
        return pltpu.make_async_copy(
            x_hbm.at[part, :, lanes(t)], x.at[t, part], x_sem.at[t, g]
        )

    for g in range(GROUPS):
        a_load(g).start()
        x_load(0, g).start()
    for t in range(1, TILES):
        for g in range(GROUPS):
            x_load(t, g).start()

    def up_copy(t, g):
        part = pl.ds(g * GROUP, GROUP)
        return remote(
            smoothed.at[part, :, lanes(t)],
            lows[t].at[part],
            up_send.at[t, g],
            up_recv.at[t, g],
            {"ax": up},
        )

    def lower_arrived(t):
        @pl.when(row > 0)
        def _():
            for g in range(GROUPS):
                up_copy(t, g).wait_recv()

    def partner(i):
        step = lax.rem(i * 5, SLOTS)
        z = lax.rem(me // 4 + step // 4, 4)
        y = lax.rem(me, 4) + lax.rem(step, 4)
        return z * 4 + lax.rem(y, 4)

    def out_copy(piece, i, first, count, t):
        j = partner(i)
        part = pl.ds(first, count)
        return remote(
            ready.at[j, part, lanes(t)],
            coarse.at[me, part, lanes(t)],
            out_send.at[piece, i],
            out_recv.at[piece, i],
            {"ay": j},
        )

    def own_copy(piece, first, count, t):
        part = pl.ds(first, count)
        return pltpu.make_async_copy(
            ready.at[me, part, lanes(t)], coarse.at[me, part, lanes(t)], own_sem.at[piece]
        )

    def slot_for(j):
        slot = jnp.int32(0)
        for s in range(SLOTS):
            slot = jnp.where(task_map[s] == j, s, slot)
        return slot

    def blocks(piece, first, count, t):
        def four(q, carry):
            for k in range(4):
                i = q * 4 + k
                j = partner(i)
                slot = slot_for(j)
                near = neighbour[slot]
                both = smoothed[slot, :, t * TILE : (t + 1) * TILE].astype(jnp.float32)
                both = both + lows[t][near].astype(jnp.float32)
                total = jnp.dot(
                    image[slot, first : first + count, :],
                    both.astype(jnp.bfloat16),
                    preferred_element_type=jnp.float32,
                )
                ready[j, pl.ds(first, count), lanes(t)] = (
                    total * (1.0 / math.sqrt(U))
                ).astype(jnp.bfloat16)

                @pl.when(i > 0)
                def _(i=i):
                    out_copy(piece, i, first, count, t).start()

            return carry

        lax.fori_loop(0, SLOTS // 4, four, 0)
        own_copy(piece, first, count, t).start()

    @pl.when(row == 0)
    def _():
        def clear(i, carry):
            for low in lows:
                low[i] = jnp.zeros((U, TILE), jnp.bfloat16)
            return carry

        lax.fori_loop(0, SLOTS, clear, 0)

    shells = (
        ((0, 0, 128, 0),),
        ((1, 0, 256, 1), (2, 128, 128, 0)),
        ((3, 0, 384, 2), (4, 256, 128, 0), (5, 256, 128, 1)),
    )
    chunks = ((0, 0, 384, 0), (1, 0, 384, 1), (2, 0, 384, 2))

    def smooth(s, carry):
        t = s // GROUPS
        g = lax.rem(s, GROUPS)

        @pl.when(t == 0)
        def _():
            a_load(g).wait()

        x_load(t, g).wait()
        cols = []
        for k in range(GROUP):
            slot = g * GROUP + k
            place = t * TILE + lax.broadcasted_iota(jnp.int32, (U, TILE), 1)
            kept = jnp.where(place < counts[slot], x[t, slot].astype(jnp.float32), 0.0)
            cols.append(kept.T.astype(jnp.bfloat16))
        for weight in omegas:
            products = [
                jnp.dot(cols[k], a[g * GROUP + k], preferred_element_type=jnp.float32)
                for k in range(GROUP)
            ]
            cols = [
                (cols[k].astype(jnp.float32) - weight * products[k]).astype(jnp.bfloat16)
                for k in range(GROUP)
            ]
        for k in range(GROUP):
            slot = g * GROUP + k
            smoothed[slot, :, lanes(t)] = cols[k].T
            applied = jnp.dot(cols[k], a[slot], preferred_element_type=jnp.float32)
            image[slot, lanes(t), :] = applied.astype(jnp.bfloat16)

        @pl.when(s == 0)
        def _():
            pl.semaphore_wait(barrier, SLOTS - 1 + 2)

        for each in range(TILES):

            @pl.when(jnp.logical_and(t == each, row < ROWS - 1))
            def _(each=each):
                up_copy(each, g).start()

            @pl.when(jnp.logical_and(s == each * GROUPS + GROUPS - 1, fast))
            def _(each=each):
                for b in range(each, each + 1):
                    lower_arrived(b)
                for piece in shells[each]:
                    blocks(*piece)

        return carry

    lax.fori_loop(0, TILES * GROUPS, smooth, 0)

    @pl.when(slow)
    def _():
        for piece in chunks:
            lower_arrived(piece[3])
            blocks(*piece)

    def finish(pieces):
        for piece, first, count, t in pieces:
            own_copy(piece, first, count, t).wait()

            def one(i, carry, piece=piece, first=first, count=count, t=t):
                out_copy(piece, i, first, count, t).wait()
                return carry

            lax.fori_loop(1, SLOTS, one, 0)

    @pl.when(fast)
    def _():
        finish(sum(shells, ()))

    @pl.when(slow)
    def _():
        finish(chunks)

    @pl.when(row < ROWS - 1)
    def _():
        for t in range(TILES):
            for g in range(GROUPS):
                up_copy(t, g).wait_send()


def body(matrices, basis_cols, mode_counts, task_map, neighbour):
    smem = pl.BlockSpec(memory_space=pltpu.SMEM)
    hbm = pl.BlockSpec(memory_space=pl.ANY)
    vmem = pl.BlockSpec(memory_space=pltpu.VMEM)
    bf16 = jnp.bfloat16
    dma = pltpu.SemaphoreType.DMA
    return pl.pallas_call(
        kernel,
        in_specs=[smem, smem, smem, hbm, hbm],
        out_specs=[vmem, vmem],
        out_shape=[
            jax.ShapeDtypeStruct((SLOTS, U, M), bf16),
            jax.ShapeDtypeStruct((SLOTS, M, M), bf16),
        ],
        scratch_shapes=[
            pltpu.VMEM((SLOTS, U, U), bf16),
            pltpu.VMEM((TILES, SLOTS, U, TILE), bf16),
            pltpu.VMEM((SLOTS, M, U), bf16),
            pltpu.VMEM((SLOTS, U, TILE), bf16),
            pltpu.VMEM((SLOTS, U, TILE), bf16),
            pltpu.VMEM((SLOTS, U, TILE), bf16),
            pltpu.VMEM((SLOTS, M, M), bf16),
            dma((GROUPS,)),
            dma((TILES, GROUPS)),
            dma((TILES, GROUPS)),
            dma((TILES, GROUPS)),
            dma((6, SLOTS)),
            dma((6, SLOTS)),
            dma((6,)),
        ],
        compiler_params=pltpu.CompilerParams(
            collective_id=0, has_side_effects=True, vmem_limit_bytes=38 << 20
        ),
    )(mode_counts, task_map, neighbour, matrices, basis_cols)


def solution(mesh):
    split = P(("ax", "ay"))

    def step(*args):
        return tuple(body(*args))

    return jax.shard_map(
        step,
        mesh=mesh,
        in_specs=(split,) * 5,
        out_specs=(split, split),
        check_vma=False,
    )
```

time: 186 us -> 102 us (0.55)
  waiting for transfers between devices: 70.1 us -> 0 us
  blocking collectives: 64.5 us -> 0 us
  Pallas kernels: 46 us -> 94.3 us
  local copies, waits for them, and re-layouts: 2.19 us -> 6.85 us
  starting transfers between devices: 1.91 us -> 0 us
    ppermute x1 -> x0, waiting for transfers between devices: 70.1 us -> none  [body(): lower_t = lax.ppermute(smoothed_t, 'ax', [(i, i + 1) for i in range(7)])]
    all_to_all x1 -> x0, blocking collectives: 64.5 us -> none  [body(): lax.all_to_all(ready, 'ay', split_axis=0, concat_axis=0, tiled=True)]
    pallas_call x2 -> x1, Pallas kernels: 46 us -> 94.3 us  [body(): pl.pallas_call(kernel, in_specs=[smem, smem, smem, hbm, hbm], out_specs=[...]
    unnamed x3 -> x8, local copies, waits for them, and re-layouts: 2.19 us -> 6.85 us
    ppermute x1 -> x0, starting transfers between devices: 1.91 us -> none  [body(): lower_t = lax.ppermute(smoothed_t, 'ax', [(i, i + 1) for i in range(7)])]
  transfers between devices with their start and end apart: 1 -> 0, of which waited for: 1 -> 0; matrix products, arithmetic and copies ran while one was open for 0% -> 0% of each run, Pallas kernels for 0% -> 0%
where the time goes in v2:
time: 102 us
  Pallas kernels  94.3 us (92%)
  local copies, waits for them, and re-layouts  6.85 us (7%)
    pallas_call x1, Pallas kernels, body(): pl.pallas_call(kernel, in_specs=[smem, smem, smem, hbm, hbm], out_specs=[...  94.3 us
    unnamed x8, local copies, waits for them, and re-layouts  6.85 us

profile of v2, /device:TPU:4, one launch (start us, length us, event | category | flops | bytes accessed | tf_op | source)
XLA Modules:
  0.0 101.8 jit_solution(8664160891920910324)
XLA Ops:
  0.6 0.0 copy-start
  0.6 0.6 copy-done
  1.3 0.0 copy-start.1
  1.3 0.7 copy-done.1
  1.9 0.0 copy-start.2
  1.9 0.7 copy-done.2
  2.6 94.3 %shard_map.68 = (bf16[16,512,384]{2,1,0:T(8,128)(2,1)S(1)}, bf16[16,384,384]{2,1,0:T(8,128)(2,1)S(1)}) custom-call(s32[16]{0:T(128)S(1)} %copy-done, s32[16]{0:T(128)S(1)} %copy-done.1, s32[16]{0:T(128)S(1)} %copy-done.2, bf16[16,512,512]{2,1,0:T(8,128)(2,1)} %a_hbm.1, bf16[16,512,384]{2,1,0:T(8,128)(2,1)} %x_hbm.1), custom_call_target="tpu_custom_call" | custom-call | tf_op jit(solution)/shard_map/pallas_call | solution.py:253
  96.9 2.7 %copy.9 = bf16[16,512,384]{2,1,0:T(8,128)(2,1)} copy(bf16[16,512,384]{2,1,0:T(8,128)(2,1)S(1)} %get-tuple-element.4) | data formatting | bytes 12582912
  99.6 2.2 %copy.10 = bf16[16,384,384]{2,1,0:T(8,128)(2,1)} copy(bf16[16,384,384]{2,1,0:T(8,128)(2,1)S(1)} %get-tuple-element.5) | data formatting | bytes 9437184
Async XLA Ops:
  0.6 0.7 copy-start
  1.3 0.7 copy-start.1
  1.9 0.7 copy-start.2

commit v3 on v2

--- a/solution.py
+++ b/solution.py
@@ -15,6 +15,7 @@
 U = 512
 M = 384
 ROWS = 8
+DETOURS = 10
 MESH = pl.DeviceIdType.MESH
 
 omegas = (0.3, 0.25, 0.2, 0.3, 0.25, 0.2)
@@ -36,15 +37,19 @@
 
 
 def kernel(
-    counts, task_map, neighbour, a_hbm, x_hbm, smoothed, coarse,
-    a, x, image, low0, low1, low2, ready,
-    a_sem, x_sem, up_send, up_recv, out_send, out_recv, own_sem,
+    counts_hbm, task_hbm, near_hbm, a_hbm, x_hbm, smoothed, coarse,
+    a, x, image, low0, low1, low2, ready, one_back, two_back,
+    counts, task_map, neighbour, slots,
+    small_sem, a_sem, x_sem, up_send, up_recv, last_send, last_recv,
+    one_recv, two_send, two_recv, end_send, out_send, out_recv, own_sem,
 ):
     lows = (low0, low1, low2)
     row = lax.axis_index("ax")
     me = lax.axis_index("ay")
     up = lax.rem(row + 1, ROWS)
-    fast = jnp.logical_or(lax.rem(row, 2) == 1, row == 0)
+    back = lax.rem(row + ROWS - 2, ROWS)
+    odd = lax.rem(row, 2) == 1
+    fast = jnp.logical_or(odd, row == 0)
     slow = jnp.logical_not(fast)
 
     barrier = pltpu.get_barrier_semaphore()
@@ -52,10 +57,19 @@
         pl.semaphore_signal(
             barrier, inc=1, device_id={"ay": lax.rem(me + k, SLOTS)}, device_id_type=MESH
         )
-    for k in (1, ROWS - 1):
+    for k in range(1, ROWS):
         pl.semaphore_signal(
             barrier, inc=1, device_id={"ax": lax.rem(row + k, ROWS)}, device_id_type=MESH
         )
+
+    smalls = [
+        pltpu.make_async_copy(src, dst, small_sem.at[k])
+        for k, (src, dst) in enumerate(
+            ((counts_hbm, counts), (task_hbm, task_map), (near_hbm, neighbour))
+        )
+    ]
+    for copy in smalls:
+        copy.start()
 
     def a_load(g):
         part = pl.ds(g * GROUP, GROUP)
@@ -74,21 +88,91 @@
         for g in range(GROUPS):
             x_load(t, g).start()
 
+    for copy in smalls:
+        copy.wait()
+    for j in range(SLOTS):
+        slot = jnp.int32(0)
+        for k in range(SLOTS):
+            slot = jnp.where(task_map[k] == j, k, slot)
+        slots[j] = slot
+
     def up_copy(t, g):
-        part = pl.ds(g * GROUP, GROUP)
-        return remote(
-            smoothed.at[part, :, lanes(t)],
-            lows[t].at[part],
+        return remote(
+            smoothed.at[pl.ds(g * GROUP, GROUP - 1), :, lanes(t)],
+            lows[t].at[pl.ds(g * GROUP, GROUP - 1)],
             up_send.at[t, g],
             up_recv.at[t, g],
             {"ax": up},
         )
+
+    def last_copy(t, g):
+        return remote(
+            smoothed.at[g * GROUP + GROUP - 1, :, lanes(t)],
+            lows[t].at[g * GROUP + GROUP - 1],
+            last_send.at[t, g],
+            last_recv.at[t, g],
+            {"ax": up},
+        )
+
+    def hop_one(t, g):
+        return remote(
+            smoothed.at[g * GROUP + GROUP - 1, :, lanes(t)],
+            one_back.at[t * GROUPS + g],
+            last_send.at[t, g],
+            one_recv.at[t * GROUPS + g],
+            {"ax": back},
+        )
+
+    def hop_two(q):
+        return remote(
+            one_back.at[q], two_back.at[q], two_send.at[q], two_recv.at[q], {"ax": back}
+        )
+
+    def hop_end(t, g):
+        q = t * GROUPS + g
+        return remote(
+            two_back.at[q],
+            lows[t].at[g * GROUP + GROUP - 1],
+            end_send.at[q],
+            last_recv.at[t, g],
+            {"ax": lax.rem(row + ROWS - 3, ROWS)},
+        )
+
+    carries_one = jnp.logical_and(odd, row != 5)
+    carries_two = jnp.logical_and(odd, row != 3)
+
+    def pass_one(q):
+        remote(
+            one_back.at[q], one_back.at[q], two_send.at[q], one_recv.at[q], {"ax": back}
+        ).wait_recv()
+        hop_two(q).start()
+
+    def pass_two(t, g):
+        q = t * GROUPS + g
+        remote(
+            two_back.at[q], two_back.at[q], end_send.at[q], two_recv.at[q], {"ax": back}
+        ).wait_recv()
+        hop_end(t, g).start()
+
+    def forward(first, second):
+        for q in first:
+
+            @pl.when(carries_one)
+            def _(q=q):
+                pass_one(q)
+
+        for q in second:
+
+            @pl.when(carries_two)
+            def _(q=q):
+                pass_two(q // GROUPS, q % GROUPS)
 
     def lower_arrived(t):
         @pl.when(row > 0)
         def _():
             for g in range(GROUPS):
                 up_copy(t, g).wait_recv()
+                last_copy(t, g).wait_recv()
 
     def partner(i):
         step = lax.rem(i * 5, SLOTS)
@@ -113,18 +197,11 @@
             ready.at[me, part, lanes(t)], coarse.at[me, part, lanes(t)], own_sem.at[piece]
         )
 
-    def slot_for(j):
-        slot = jnp.int32(0)
-        for s in range(SLOTS):
-            slot = jnp.where(task_map[s] == j, s, slot)
-        return slot
-
     def blocks(piece, first, count, t):
         def four(q, carry):
+            totals = []
             for k in range(4):
-                i = q * 4 + k
-                j = partner(i)
-                slot = slot_for(j)
+                slot = slots[partner(q * 4 + k)]
                 near = neighbour[slot]
                 both = smoothed[slot, :, t * TILE : (t + 1) * TILE].astype(jnp.float32)
                 both = both + lows[t][near].astype(jnp.float32)
@@ -133,14 +210,16 @@
                     both.astype(jnp.bfloat16),
                     preferred_element_type=jnp.float32,
                 )
-                ready[j, pl.ds(first, count), lanes(t)] = (
-                    total * (1.0 / math.sqrt(U))
-                ).astype(jnp.bfloat16)
-
-                @pl.when(i > 0)
-                def _(i=i):
-                    out_copy(piece, i, first, count, t).start()
-
+                totals.append((total * (1.0 / math.sqrt(U))).astype(jnp.bfloat16))
+            for k in range(4):
+                ready[partner(q * 4 + k), pl.ds(first, count), lanes(t)] = totals[k]
+
+            @pl.when(q > 0)
+            def _():
+                out_copy(piece, q * 4, first, count, t).start()
+
+            for k in range(1, 4):
+                out_copy(piece, q * 4 + k, first, count, t).start()
             return carry
 
         lax.fori_loop(0, SLOTS // 4, four, 0)
@@ -160,7 +239,19 @@
         ((1, 0, 256, 1), (2, 128, 128, 0)),
         ((3, 0, 384, 2), (4, 256, 128, 0), (5, 256, 128, 1)),
     )
-    chunks = ((0, 0, 384, 0), (1, 0, 384, 1), (2, 0, 384, 2))
+    chunks = ((0, 0, 256, 0), (1, 256, 128, 0), (2, 0, 384, 1), (3, 0, 384, 2))
+    passes = (
+        (2, (0,), ()),
+        (3, (1,), ()),
+        (4, (), (0,)),
+        (5, (2,), (1,)),
+        (6, (3,), ()),
+        (7, (), (2, 3)),
+        (8, (4,), ()),
+        (9, (5,), (4,)),
+        (10, (), (5,)),
+        (11, (6, 7), (6,)),
+    )
 
     def smooth(s, carry):
         t = s // GROUPS
@@ -194,18 +285,39 @@
 
         @pl.when(s == 0)
         def _():
-            pl.semaphore_wait(barrier, SLOTS - 1 + 2)
+            pl.semaphore_wait(barrier, SLOTS - 1 + ROWS - 1)
 
         for each in range(TILES):
 
             @pl.when(jnp.logical_and(t == each, row < ROWS - 1))
             def _(each=each):
                 up_copy(each, g).start()
+                around = jnp.logical_and(odd, s < DETOURS)
+
+                @pl.when(around)
+                def _():
+                    hop_one(each, g).start()
+
+                @pl.when(jnp.logical_not(around))
+                def _():
+                    last_copy(each, g).start()
+
+        for at, first, second in passes:
+
+            @pl.when(jnp.logical_and(s == at, odd))
+            def _(first=first, second=second):
+                forward(first, second)
+
+        @pl.when(jnp.logical_and(s == 8, slow))
+        def _():
+            lower_arrived(0)
+            blocks(*chunks[0])
+
+        for each in range(TILES):
 
             @pl.when(jnp.logical_and(s == each * GROUPS + GROUPS - 1, fast))
             def _(each=each):
-                for b in range(each, each + 1):
-                    lower_arrived(b)
+                lower_arrived(each)
                 for piece in shells[each]:
                     blocks(*piece)
 
@@ -213,9 +325,13 @@
 
     lax.fori_loop(0, TILES * GROUPS, smooth, 0)
 
+    for q in range(7, DETOURS + 1):
+        forward((q + 1,) if q + 1 < DETOURS else (), (q,) if q < DETOURS else ())
+
     @pl.when(slow)
     def _():
-        for piece in chunks:
+        blocks(*chunks[1])
+        for piece in chunks[2:]:
             lower_arrived(piece[3])
             blocks(*piece)
 
@@ -242,17 +358,27 @@
         for t in range(TILES):
             for g in range(GROUPS):
                 up_copy(t, g).wait_send()
+                last_copy(t, g).wait_send()
+
+    @pl.when(carries_one)
+    def _():
+        for q in range(DETOURS):
+            hop_two(q).wait_send()
+
+    @pl.when(carries_two)
+    def _():
+        for q in range(DETOURS):
+            hop_end(q // GROUPS, q % GROUPS).wait_send()
 
 
 def body(matrices, basis_cols, mode_counts, task_map, neighbour):
-    smem = pl.BlockSpec(memory_space=pltpu.SMEM)
-    hbm = pl.BlockSpec(memory_space=pl.ANY)
+    hbm = pl.BlockSpec(memory_space=pltpu.HBM)
     vmem = pl.BlockSpec(memory_space=pltpu.VMEM)
     bf16 = jnp.bfloat16
     dma = pltpu.SemaphoreType.DMA
     return pl.pallas_call(
         kernel,
-        in_specs=[smem, smem, smem, hbm, hbm],
+        in_specs=[hbm] * 5,
         out_specs=[vmem, vmem],
         out_shape=[
             jax.ShapeDtypeStruct((SLOTS, U, M), bf16),
@@ -266,10 +392,23 @@
             pltpu.VMEM((SLOTS, U, TILE), bf16),
             pltpu.VMEM((SLOTS, U, TILE), bf16),
             pltpu.VMEM((SLOTS, M, M), bf16),
+            pltpu.VMEM((TILES * GROUPS, U, TILE), bf16),
+            pltpu.VMEM((TILES * GROUPS, U, TILE), bf16),
+            pltpu.SMEM((SLOTS,), jnp.int32),
+            pltpu.SMEM((SLOTS,), jnp.int32),
+            pltpu.SMEM((SLOTS,), jnp.int32),
+            pltpu.SMEM((SLOTS,), jnp.int32),
+            dma((3,)),
             dma((GROUPS,)),
             dma((TILES, GROUPS)),
             dma((TILES, GROUPS)),
             dma((TILES, GROUPS)),
+            dma((TILES, GROUPS)),
+            dma((TILES, GROUPS)),
+            dma((TILES * GROUPS,)),
+            dma((TILES * GROUPS,)),
+            dma((TILES * GROUPS,)),
+            dma((TILES * GROUPS,)),
             dma((6, SLOTS)),
             dma((6, SLOTS)),
             dma((6,)),
@@ -277,7 +416,14 @@
         compiler_params=pltpu.CompilerParams(
             collective_id=0, has_side_effects=True, vmem_limit_bytes=38 << 20
         ),
-    )(mode_counts, task_map, neighbour, matrices, basis_cols)
+    )(
+        *(
+            pltpu.with_memory_space_constraint(small, pltpu.HBM)
+            for small in (mode_counts, task_map, neighbour)
+        ),
+        matrices,
+        basis_cols,
+    )
 
 
 def solution(mesh):

time: 102 us -> 94.8 us (0.929)
  Pallas kernels: 94.3 us -> 89.1 us
  local copies, waits for them, and re-layouts: 6.85 us -> 4.89 us
    pallas_call x1, Pallas kernels: 94.3 us -> 89.1 us  [body(): pl.pallas_call(kernel, in_specs=[hbm] * 5, out_specs=[vmem, vmem], out_sh...]
    unnamed x8 -> x2, local copies, waits for them, and re-layouts: 6.85 us -> 4.89 us
where the time goes in v3:
time: 94.8 us; the launch traced here: 94.7 us
  Pallas kernels  89.1 us (94%)
  local copies, waits for them, and re-layouts  4.89 us (5%)
    pallas_call x1, Pallas kernels, body(): pl.pallas_call(kernel, in_specs=[hbm] * 5, out_specs=[vmem, vmem], out_sh...  89.1 us
    unnamed x2, local copies, waits for them, and re-layouts  4.89 us

profile of v3, /device:TPU:4, one launch (start us, length us, event | category | flops | bytes accessed | tf_op | source)
XLA Modules:
  0.0 94.7 jit_solution(5536499443189705289)
XLA Ops:
  0.6 89.1 %shard_map.68 = (bf16[16,512,384]{2,1,0:T(8,128)(2,1)S(1)}, bf16[16,384,384]{2,1,0:T(8,128)(2,1)S(1)}) custom-call(s32[16]{0:T(128)} %counts_hbm.1, s32[16]{0:T(128)} %task_hbm.1, s32[16]{0:T(128)} %near_hbm.1, bf16[16,512,512]{2,1,0:T(8,128)(2,1)} %a_hbm.1, bf16[16,512,384]{2,1,0:T(8,128)(2,1)} %x_hbm.1), custom_call_target="tpu_custom_call" | custom-call | tf_op jit(solution)/shard_map/pallas_call | solution.py:379
  89.8 2.7 %copy.9 = bf16[16,512,384]{2,1,0:T(8,128)(2,1)} copy(bf16[16,512,384]{2,1,0:T(8,128)(2,1)S(1)} %get-tuple-element.4) | data formatting | bytes 12582912
  92.5 2.2 %copy.10 = bf16[16,384,384]{2,1,0:T(8,128)(2,1)} copy(bf16[16,384,384]{2,1,0:T(8,128)(2,1)S(1)} %get-tuple-element.5) | data formatting | bytes 9437184

commit v4 on v3

--- a/solution.py
+++ b/solution.py
@@ -15,7 +15,7 @@
 U = 512
 M = 384
 ROWS = 8
-DETOURS = 10
+DETOURS = 8
 MESH = pl.DeviceIdType.MESH
 
 omegas = (0.3, 0.25, 0.2, 0.3, 0.25, 0.2)
@@ -90,11 +90,6 @@
 
     for copy in smalls:
         copy.wait()
-    for j in range(SLOTS):
-        slot = jnp.int32(0)
-        for k in range(SLOTS):
-            slot = jnp.where(task_map[k] == j, k, slot)
-        slots[j] = slot
 
     def up_copy(t, g):
         return remote(
@@ -175,7 +170,7 @@
                 last_copy(t, g).wait_recv()
 
     def partner(i):
-        step = lax.rem(i * 5, SLOTS)
+        step = lax.rem(i * 7, SLOTS)
         z = lax.rem(me // 4 + step // 4, 4)
         y = lax.rem(me, 4) + lax.rem(step, 4)
         return z * 4 + lax.rem(y, 4)
@@ -265,9 +260,10 @@
         cols = []
         for k in range(GROUP):
             slot = g * GROUP + k
-            place = t * TILE + lax.broadcasted_iota(jnp.int32, (U, TILE), 1)
-            kept = jnp.where(place < counts[slot], x[t, slot].astype(jnp.float32), 0.0)
-            cols.append(kept.T.astype(jnp.bfloat16))
+            place = t * TILE + lax.broadcasted_iota(jnp.int32, (TILE, U), 0)
+            given = x[t, slot].T.astype(jnp.float32)
+            kept = jnp.where(place < counts[slot], given, 0.0)
+            cols.append(kept.astype(jnp.bfloat16))
         for weight in omegas:
             products = [
                 jnp.dot(cols[k], a[g * GROUP + k], preferred_element_type=jnp.float32)
@@ -285,6 +281,11 @@
 
         @pl.when(s == 0)
         def _():
+            for j in range(SLOTS):
+                slot = jnp.int32(0)
+                for k in range(SLOTS):
+                    slot = jnp.where(task_map[k] == j, k, slot)
+                slots[j] = slot
             pl.semaphore_wait(barrier, SLOTS - 1 + ROWS - 1)
 
         for each in range(TILES):
@@ -426,11 +427,39 @@
     )
 
 
+def place_kernel(s_in, c_in, s_out, c_out, sem):
+    copies = []
+    for k in range(4):
+        part = pl.ds(k * GROUP, GROUP)
+        copies.append(pltpu.make_async_copy(s_in.at[part], s_out.at[part], sem.at[0, k]))
+        copies.append(pltpu.make_async_copy(c_in.at[part], c_out.at[part], sem.at[1, k]))
+    for copy in copies:
+        copy.start()
+    for copy in copies:
+        copy.wait()
+
+
+def place(smoothed, coarse):
+    inside = pl.BlockSpec(memory_space=pltpu.VMEM)
+    outside = pl.BlockSpec(memory_space=pltpu.HBM)
+    return pl.pallas_call(
+        place_kernel,
+        in_specs=[inside] * 2,
+        out_specs=[outside] * 2,
+        out_shape=[
+            jax.ShapeDtypeStruct(smoothed.shape, smoothed.dtype),
+            jax.ShapeDtypeStruct(coarse.shape, coarse.dtype),
+        ],
+        scratch_shapes=[pltpu.SemaphoreType.DMA((2, 4))],
+        compiler_params=pltpu.CompilerParams(vmem_limit_bytes=1 << 20),
+    )(smoothed, coarse)
+
+
 def solution(mesh):
     split = P(("ax", "ay"))
 
     def step(*args):
-        return tuple(body(*args))
+        return tuple(place(*body(*args)))
 
     return jax.shard_map(
         step,

time: 94.8 us -> 92.3 us (0.974)
  local copies, waits for them, and re-layouts: 4.89 us -> 0 us
  Pallas kernels: 89.1 us -> 91.3 us
    unnamed x2 -> x0, local copies, waits for them, and re-layouts: 4.89 us -> none
    pallas_call x0 -> x1, Pallas kernels: none -> 4.16 us  [place(): pl.pallas_call(place_kernel, in_specs=[inside] * 2, out_specs=[outside] *...]
    pallas_call x1, Pallas kernels: 89.1 us -> 87.1 us  [body(): pl.pallas_call(kernel, in_specs=[hbm] * 5, out_specs=[vmem, vmem], out_sh...]
where the time goes in v4:
time: 92.3 us; the launch traced here: 91.9 us
  Pallas kernels  91.3 us (99%)
    pallas_call x1, Pallas kernels, body(): pl.pallas_call(kernel, in_specs=[hbm] * 5, out_specs=[vmem, vmem], out_sh...  87.1 us
    pallas_call x1, Pallas kernels, place(): pl.pallas_call(place_kernel, in_specs=[inside] * 2, out_specs=[outside] *...  4.16 us

profile of v4, /device:TPU:4, one launch (start us, length us, event | category | flops | bytes accessed | tf_op | source)
XLA Modules:
  0.0 91.9 jit_solution(6716888702090449140)
XLA Ops:
  0.6 87.1 %shard_map.68 = (bf16[16,512,384]{2,1,0:T(8,128)(2,1)S(1)}, bf16[16,384,384]{2,1,0:T(8,128)(2,1)S(1)}) custom-call(s32[16]{0:T(128)} %counts_hbm.1, s32[16]{0:T(128)} %task_hbm.1, s32[16]{0:T(128)} %near_hbm.1, bf16[16,512,512]{2,1,0:T(8,128)(2,1)} %a_hbm.1, bf16[16,512,384]{2,1,0:T(8,128)(2,1)} %x_hbm.1), custom_call_target="tpu_custom_call" | custom-call | tf_op jit(solution)/shard_map/pallas_call | solution.py:380
  87.8 4.2 %shard_map.69 = (bf16[16,512,384]{2,1,0:T(8,128)(2,1)}, bf16[16,384,384]{2,1,0:T(8,128)(2,1)}) custom-call(bf16[16,512,384]{2,1,0:T(8,128)(2,1)S(1)} %get-tuple-element.4.s_in, bf16[16,384,384]{2,1,0:T(8,128)(2,1)S(1)} %get-tuple-element.5.c_in), custom_call_target="tpu_custom_call" | custom-call | tf_op jit(solution)/shard_map/pallas_call | solution.py:445

commit v5 on v4

--- a/solution.py
+++ b/solution.py
@@ -16,6 +16,7 @@
 M = 384
 ROWS = 8
 DETOURS = 8
+AHEAD = 2
 MESH = pl.DeviceIdType.MESH
 
 omegas = (0.3, 0.25, 0.2, 0.3, 0.25, 0.2)
@@ -81,12 +82,9 @@
             x_hbm.at[part, :, lanes(t)], x.at[t, part], x_sem.at[t, g]
         )
 
-    for g in range(GROUPS):
+    for g in range(AHEAD):
         a_load(g).start()
         x_load(0, g).start()
-    for t in range(1, TILES):
-        for g in range(GROUPS):
-            x_load(t, g).start()
 
     for copy in smalls:
         copy.wait()
@@ -257,6 +255,16 @@
             a_load(g).wait()
 
         x_load(t, g).wait()
+        later = s + AHEAD
+
+        @pl.when(later < GROUPS)
+        def _():
+            a_load(later).start()
+
+        @pl.when(later < TILES * GROUPS)
+        def _():
+            x_load(later // GROUPS, lax.rem(later, GROUPS)).start()
+
         cols = []
         for k in range(GROUP):
             slot = g * GROUP + k

time: 92.3 us -> 91.2 us (0.988)
  Pallas kernels: 91.3 us -> 90.2 us
    pallas_call x1, Pallas kernels: 87.1 us -> 86 us  [body(): pl.pallas_call(kernel, in_specs=[hbm] * 5, out_specs=[vmem, vmem], out_sh...]
where the time goes in v5:
time: 91.2 us; the launch traced here: 90.8 us
  Pallas kernels  90.2 us (99%)
    pallas_call x1, Pallas kernels, body(): pl.pallas_call(kernel, in_specs=[hbm] * 5, out_specs=[vmem, vmem], out_sh...  86 us
    pallas_call x1, Pallas kernels, place(): pl.pallas_call(place_kernel, in_specs=[inside] * 2, out_specs=[outside] *...  4.16 us

profile of v5, /device:TPU:4, one launch (start us, length us, event | category | flops | bytes accessed | tf_op | source)
XLA Modules:
  0.0 90.8 jit_solution(1893132948035615077)
XLA Ops:
  0.6 86.0 %shard_map.68 = (bf16[16,512,384]{2,1,0:T(8,128)(2,1)S(1)}, bf16[16,384,384]{2,1,0:T(8,128)(2,1)S(1)}) custom-call(s32[16]{0:T(128)} %counts_hbm.1, s32[16]{0:T(128)} %task_hbm.1, s32[16]{0:T(128)} %near_hbm.1, bf16[16,512,512]{2,1,0:T(8,128)(2,1)} %a_hbm.1, bf16[16,512,384]{2,1,0:T(8,128)(2,1)} %x_hbm.1), custom_call_target="tpu_custom_call" | custom-call | tf_op jit(solution)/shard_map/pallas_call | solution.py:388
  86.7 4.2 %shard_map.69 = (bf16[16,512,384]{2,1,0:T(8,128)(2,1)}, bf16[16,384,384]{2,1,0:T(8,128)(2,1)}) custom-call(bf16[16,512,384]{2,1,0:T(8,128)(2,1)S(1)} %get-tuple-element.4.s_in, bf16[16,384,384]{2,1,0:T(8,128)(2,1)S(1)} %get-tuple-element.5.c_in), custom_call_target="tpu_custom_call" | custom-call | tf_op jit(solution)/shard_map/pallas_call | solution.py:453
